TPU v7x, 256 devices: a whole 4x4x8 slice. The times are simulated.
256 devices in a mesh: lat: 2 (over x_hi), dp: 64 (over z, y, core), exp: 2 (over x_lo).
Axes of the slice: x: 4 (x_hi: 2, x_lo: 2; x = x_hi * 2 + x_lo), y: 4, z: 8, core: 2. Of those that a mesh axis runs over, the one named last changes fastest.
Arguments:
- images: bfloat16 [128, 32, 256, 192], P(('dp', 'exp'), 'lat'), may hold values from -6 to 6
- cotangent: bfloat16 [128, 32, 256, 192], P(('dp', 'exp'), 'lat'), may hold values from -0.0625 to 0.0625
- labels: int32 [128, 32, 2, 1], P(('dp', 'exp'), 'lat'), may hold values from 0 to 15; in each aligned block of 32 rows (0 to 31, 32 to 63, ..., all dimensions but the last counted through in order) at most 3 rows name the same one
- dw_kernel: float32 [7, 7, 192], replicated, may hold values from -0.875 to 0.875
- ln_gain: float32 [192], replicated, may hold values from 0.5 to 2
- w_expand: bfloat16 [192, 768], replicated, may hold values from -0.4375 to 0.4375
- w_reduce: bfloat16 [768, 192], replicated, may hold values from -0.21875 to 0.21875
- exp_in: bfloat16 [16, 192, 768], P('exp'), may hold values from -0.4375 to 0.4375
- exp_out: bfloat16 [16, 768, 192], P('exp'), may hold values from -0.21875 to 0.21875
Outputs:
- output: bfloat16 [128, 32, 256, 192], P(('dp', 'exp'), 'lat')
- grad_in: float32 [16, 192, 768], P('exp')
- grad_out: float32 [16, 768, 192], P('exp')
Inputs may be any that keep to these rules, and one draw needn't show every extreme that they name: `labels`: among the 32 row blocks of one device (aligned runs of 32 blocks in the order clip, row, block), no class is named more than 3 times, a bound that some block reaches.
All inputs are finite; a program needn't handle non-finite values.
Results may differ from a plain program's by a relative error of at most 0.0072.
Values may be sent and summed in bfloat16 or wider, within the bound.
A program may use at most 128 MiB of HBM per device.

v0:
```python
import jax
import jax.numpy as jnp
from jax import lax
from jax.sharding import PartitionSpec as P

EXPERTS = 16
BLOCK = 128
CAP = 3


def with_halo(block, sides, width):
    for axis, dim in sides:
        count = lax.axis_size(axis)
        forward = [(i, i + 1) for i in range(count - 1)]
        backward = [(target, source) for source, target in forward]
        low = lax.ppermute(
            lax.slice_in_dim(block, block.shape[dim] - width, None, axis=dim), axis, forward
        )
        high = lax.ppermute(lax.slice_in_dim(block, 0, width, axis=dim), axis, backward)
        block = jnp.concatenate([low, block, high], axis=dim)
    return block


def gelu_slope(values):
    return (
        0.5 * (1.0 + lax.erf(values * 0.7071067811865476))
        + values * jnp.exp(-0.5 * values * values) * 0.3989422804014327
    )


def depthwise(padded, kernel):
    row_count = padded.shape[1] - 6
    col_count = padded.shape[2] - 6
    summed = jnp.zeros((padded.shape[0], row_count, col_count, padded.shape[3]), jnp.float32)
    for row_off in range(7):
        for col_off in range(7):
            window = padded[:, row_off : row_off + row_count, col_off : col_off + col_count, :]
            summed = summed + window.astype(jnp.float32) * kernel[row_off, col_off]
    return summed


def widen(picture):
    return jnp.pad(picture, ((0, 0), (0, 0), (3, 3), (0, 0)))


def dense_block(images, smoothed, ln_gain, w_expand, w_reduce):
    channels = images.shape[-1]
    channel_mean = jnp.mean(smoothed, axis=-1, keepdims=True)
    centered = smoothed - channel_mean
    variance = jnp.mean(centered * centered, axis=-1, keepdims=True)
    normed = (centered * lax.rsqrt(variance + 1e-06) * ln_gain).astype(jnp.bfloat16)
    flat_normed = normed.reshape(-1, channels)
    expanded = jnp.dot(flat_normed, w_expand, preferred_element_type=jnp.float32)
    active = jax.nn.gelu(expanded, approximate=False).astype(jnp.bfloat16)
    reduced = jnp.dot(active, w_reduce, preferred_element_type=jnp.float32)
    dense_out = images.reshape(-1, channels).astype(jnp.float32) + reduced
    return dense_out.astype(jnp.bfloat16).reshape(images.shape)


def expert_pass(inputs, grads_in, w_in, w_out):
    pre_act = jnp.dot(inputs, w_in, preferred_element_type=jnp.float32)
    hidden = jax.nn.gelu(pre_act, approximate=False).astype(jnp.bfloat16)
    outputs = jnp.dot(hidden, w_out, preferred_element_type=jnp.float32).astype(jnp.bfloat16)
    grad_out = jnp.dot(hidden.T, grads_in, preferred_element_type=jnp.float32)
    back_prop = jnp.dot(grads_in, w_out.T, preferred_element_type=jnp.float32)
    scaled = (back_prop * gelu_slope(pre_act)).astype(jnp.bfloat16)
    grad_in = jnp.dot(inputs.T, scaled, preferred_element_type=jnp.float32)
    return (outputs, grad_in, grad_out)


def body(images, cotangent, labels, dw_kernel, ln_gain, w_expand, w_reduce, exp_in, exp_out):
    channels = images.shape[-1]
    padded = with_halo(images, (("lat", 1),), 3)
    smoothed = depthwise(widen(padded), dw_kernel)
    dense_out = dense_block(images, smoothed, ln_gain, w_expand, w_reduce)
    block_width = BLOCK * channels
    blocks = dense_out.reshape(-1, block_width)
    grad_blocks = cotangent.reshape(-1, block_width)
    flat_labels = labels.reshape(-1)
    members = (flat_labels[:, None] == jnp.arange(EXPERTS, dtype=jnp.int32)[None, :]).astype(
        jnp.int32
    )
    before = jnp.sum(jnp.cumsum(members, axis=0) * members, axis=1) - 1
    slot_of = flat_labels * CAP + before
    placer = (jnp.arange(EXPERTS * CAP, dtype=jnp.int32)[:, None] == slot_of[None, :]).astype(
        jnp.bfloat16
    )
    outgoing = (
        jnp.dot(placer, blocks, preferred_element_type=jnp.float32)
        .astype(jnp.bfloat16)
        .reshape(EXPERTS, CAP, block_width)
    )
    outgoing_grads = (
        jnp.dot(placer, grad_blocks, preferred_element_type=jnp.float32)
        .astype(jnp.bfloat16)
        .reshape(EXPERTS, CAP, block_width)
    )

    def run_expert(expert_items):
        inputs, grads_in, w_in, w_out = expert_items
        outputs, grad_in, grad_out = expert_pass(
            inputs.reshape(-1, channels), grads_in.reshape(-1, channels), w_in, w_out
        )
        return (outputs.reshape(inputs.shape), grad_in, grad_out)

    arrived, arrived_grads = (
        lax.all_to_all(outgoing, "exp", split_axis=0, concat_axis=1, tiled=True),
        lax.all_to_all(outgoing_grads, "exp", split_axis=0, concat_axis=1, tiled=True),
    )
    results, grad_in, grad_out = lax.map(run_expert, (arrived, arrived_grads, exp_in, exp_out))
    returned = lax.all_to_all(results, "exp", split_axis=1, concat_axis=0, tiled=True)
    grad_in, grad_out = lax.psum((grad_in, grad_out), ("lat", "dp"))
    expert_out = jnp.dot(
        placer.T, returned.reshape(EXPERTS * CAP, block_width), preferred_element_type=jnp.float32
    ).astype(jnp.bfloat16)
    output = (
        dense_out.astype(jnp.float32) + expert_out.reshape(dense_out.shape).astype(jnp.float32)
    ).astype(jnp.bfloat16)
    return (output, grad_in, grad_out)


def solution(mesh):
    in_specs = (
        P(("dp", "exp"), "lat", None, None),
        P(("dp", "exp"), "lat", None, None),
        P(("dp", "exp"), "lat", None, None),
        P(),
        P(),
        P(),
        P(),
        P("exp", None, None),
        P("exp", None, None),
    )
    out_specs = (P(("dp", "exp"), "lat", None, None), P("exp", None, None), P("exp", None, None))
    return jax.shard_map(body, mesh=mesh, in_specs=in_specs, out_specs=out_specs, check_vma=False)
```

profile of v0, /device:TPU:7, one launch (start us, length us, event | category | flops | bytes accessed | tf_op | source)
XLA Modules:
  0.0 1624.9 jit_solution(9651882044922824037)
XLA Ops:
  10.3 5.5 collective-permute-start.1
  17.0 2.7 copy.24
  19.8 3.2 reshape.261
  23.0 2.2 convolution_convert_fusion.1
  25.1 2.5 reshape.262
  27.6 5.9 all-to-all-start.1
  36.3 2.2 fusion.69
  38.6 26.9 %fusion.104 = (f32[16,256]{1,0:T(8,128)S(1)}, f32[1,16,256,192]{2,3,1,0:T(8,128)S(1)}) fusion(f32[192]{0:T(256)S(1)} %bitcast.170, bf16[1,22,262,192]{2,3,1,0:T(8,128)(2,1)S(1)} %fusion.69, f32[192]{0:T(256)S(1)} %bitcast.171, f32[192]{0:T(256)S(1)} %bitcast.143, f32[192]{0:T(256)S(1)} %bitcast.144, ...), kind=kLoop, calls=%fused_computation.138 | loop fusion | flops 115601408 | bytes 80270080 | tf_op jit(solution)/shard_map/reduce_sum | solution.py:48
  68.6 42.4 %fusion.60 = bf16[4096,192]{0,1:T(8,128)(2,1)} fusion(f32[4096,192]{0,1:T(8,128)S(1)} %bitcast.140, bf16[768,192]{0,1:T(8,128)(2,1)S(1)} %copy-done, bf16[4096,192]{0,1:T(8,128)(2,1)} %bitcast.141, bf16[192,768]{1,0:T(8,128)(2,1)} %param.16), kind=kOutput, calls=%fused_computation.83 | convolution fusion | flops 2621964288 | bytes 6881280 | tf_op jit(solution)/shard_map/dot_general | solution.py:55
  111.0 3.2 copy.22
  114.1 3.2 reshape_reshape.3
  117.3 2.2 convolution_convert_fusion.2
  119.5 2.5 reshape.260
  121.9 4.0 all-to-all-start
  126.0 3.6 copy.25
  129.6 2.9 copy.27
  132.5 27.1 %all-to-all-done = bf16[16,3,24576]{2,1,0:T(4,128)(2,1)S(1)} async-done(((bf16[16,3,24576]{2,1,0:T(4,128)(2,1)}), bf16[16,3,24576]{2,1,0:T(4,128)(2,1)S(1)}, u32[]{:S(2)}, u32[]{:S(2)}) %all-to-all-start) | async-done | bytes 2359328 | tf_op jit(solution)/shard_map/all_to_all | solution.py:107
  161.4 3.1 copy.26
  164.4 147.7 %while.14 = (s32[]{:T(128)}, bf16[8,6,24576]{2,1,0:T(8,128)(2,1)}, f32[8,192,768]{2,1,0:T(8,128)}, f32[8,768,192]{1,2,0:T(8,128)}, bf16[8,6,24576]{2,1,0:T(8,128...) while((s32[]{:T(128)}, bf16[8,6,24576]{2,1,0:T(8,128)(2,1)}, ...), condition=%wide.region_5.6_spmd, body=%wide.region_4.5_spmd.sunk | while | flops 1176846336 | bytes 16123001 | solution.py:110
  166.3 7.3 fusion.141
  178.1 3.9 fusion.142
  184.7 7.3 fusion.141
  196.5 3.9 fusion.142
  203.1 7.3 fusion.141
  214.9 3.9 fusion.142
  221.6 7.3 fusion.141
  233.3 3.9 fusion.142
  240.0 7.3 fusion.141
  251.8 3.9 fusion.142
  258.4 7.3 fusion.141
  270.2 3.9 fusion.142
  276.8 7.3 fusion.141
  288.6 3.9 fusion.142
  295.2 7.3 fusion.141
  307.0 3.9 fusion.142
  314.0 2.7 copy.28
  316.7 6.2 all-to-all-start.2
  322.9 3.1 copy.32
  326.0 21.4 %all-to-all-done.2 = bf16[8,6,24576]{2,0,1:T(8,128)(2,1)} async-done(((bf16[8,6,24576]{2,0,1:T(8,128)(2,1)}), bf16[8,6,24576]{2,0,1:T(8,128)(2,1)}, u32[]{:S(2)}, u32[]{:S(2)}) %all-to-all-start.2) | async-done | bytes 2359328 | tf_op jit(solution)/shard_map/all_to_all | solution.py:111
  347.4 3.7 copy.29
  351.1 3.0 reshape.263
  354.1 2.3 fusion.43
  356.4 3.3 reshape.266
  359.6 4.1 add_convert_fusion
  363.7 2.3 copy.31
  366.0 1244.7 %all-reduce.4.cloned.1.call-done = (f32[8,192,768]{2,1,0:T(8,128)}, f32[8,768,192]{1,2,0:T(8,128)}) async-done(((f32[8,192,768]{2,1,0:T(8,128)}, f32[8,768,192]{1,2,0:T(8,128)}), (f32[8,192,768]{2,1,0:T(8,128)}, f32[8,768,192]{1,2,0:T(8,128)})) %all-reduce.4.cloned.1.call-update) | async-done | bytes 9437200 | tf_op jit(solution)/shard_map/psum | solution.py:112
  1610.7 5.0 copy.60
  1615.7 2.2 copy.61
  (114 shorter events, 71.3 us)
Async XLA Ops:
  7.2 60.9 %copy-start = (bf16[768,192]{0,1:T(8,128)(2,1)S(1)}, bf16[768,192]{0,1:T(8,128)(2,1)}, u32[]{:S(2)}) copy-start(bf16[768,192]{0,1:T(8,128)(2,1)} %param.17) | copy-start | bytes 884740
  9.0 24.6 %collective-permute-start = (bf16[1,3,256,192]{2,3,1,0:T(8,128)(2,1)}, bf16[1,3,256,192]{2,3,1,0:T(8,128)(2,1)S(1)}, u32[]{:S(2)}, u32[]{:S(2)}) collective-permute-start(bf16[1,3,256,192]{2,3,1,0:T(8,128)(2,1)} %get-tuple-element.88), channel_id=1, source_target_pairs={{0,128},{1,129},{2,130},{3,131},{4,132},{5,133},{6,134},{7,135},{8... | collective-permute-start | bytes 884744 | tf_op jit(solution)/shard_map/ppermute | solution.py:16
  10.3 26.0 %collective-permute-start.1 = (bf16[1,3,256,192]{2,3,1,0:T(8,128)(2,1)S(1)}, bf16[1,3,256,192]{2,3,1,0:T(8,128)(2,1)S(1)}, u32[]{:S(2)}, u32[]{:S(2)}) collective-permute-start(bf16[1,3,256,192]{2,3,1,0:T(8,128)(2,1)S(1)} %get-tuple-element.89), channel_id=1, source_target_pairs={{128,0},{129,1},{130,2},{131,3},{132,4},{133,5},{134,6},{135,7},{1... | collective-permute-start | bytes 884744 | tf_op jit(solution)/shard_map/ppermute | solution.py:19
  27.6 5.9 copy-start.6
  27.6 6.0 copy-start.2
  27.6 94.3 %all-to-all-start.1 = ((bf16[16,3,24576]{2,1,0:T(4,128)(2,1)}), bf16[16,3,24576]{2,1,0:T(4,128)(2,1)}, u32[]{:S(2)}, u32[]{:S(2)}) async-start(bf16[16,3,24576]{2,1,0:T(4,128)(2,1)} %reshape.262), calls=%async_computation.1 | async-start | bytes 6291456 | tf_op jit(solution)/shard_map/all_to_all | solution.py:108
  65.5 0.7 copy-start.7
  66.2 2.4 copy-start.4
  121.9 37.7 %all-to-all-start = ((bf16[16,3,24576]{2,1,0:T(4,128)(2,1)}), bf16[16,3,24576]{2,1,0:T(4,128)(2,1)S(1)}, u32[]{:S(2)}, u32[]{:S(2)}) async-start(bf16[16,3,24576]{2,1,0:T(4,128)(2,1)} %reshape.260), calls=%async_computation | async-start | bytes 6291456 | tf_op jit(solution)/shard_map/all_to_all | solution.py:107
  125.9 1484.7 %all-reduce.4.cloned.1.call-start = ((), (), s32[]{:S(2)}) async-start(), calls=%async_computation.3 | async-start | bytes 18874368 | tf_op jit(solution)/shard_map/psum | solution.py:112
  312.1 1.9 copy-start.5
  316.7 6.2 copy-start.3
  316.7 30.6 %all-to-all-start.2 = ((bf16[8,6,24576]{2,0,1:T(8,128)(2,1)}), bf16[8,6,24576]{2,0,1:T(8,128)(2,1)}, u32[]{:S(2)}, u32[]{:S(2)}) async-start(bf16[8,6,24576]{2,0,1:T(8,128)(2,1)} %copy.28), calls=%async_computation.2 | async-start | bytes 4718592 | tf_op jit(solution)/shard_map/all_to_all | solution.py:111
  1610.7 5.0 slice-start
  1610.7 5.0 slice-start.1
  1610.7 7.2 copy-start.1
Sparse Core Ops, SparseCore 0:
  312.3 1298.3 all-reduce.3
where the time goes:
time: 1640 us; the launch traced here: 1620 us
  waiting for transfers between devices  1290 us (79%)
  matrix products  161 us (10%)
  local copies, waits for them, and re-layouts  98.1 us (6%)
  other arithmetic  35 us (2%)
  starting transfers between devices  22.9 us (1%)
    psum x1, waiting for transfers between devices, body(): grad_in, grad_out = lax.psum((grad_in, grad_out), ('lat', 'dp'))  1240 us
    dot_general x8, matrix products, expert_pass(): pre_act = jnp.dot(inputs, w_in, preferred_element_type=jnp.float32)  58.5 us
    dot_general x1, matrix products, dense_block(): reduced = jnp.dot(active, w_reduce, preferred_element_type=jnp.float32)  42.4 us
  transfers between devices with their start and end apart: 6, of which 3 were waited for; matrix products, arithmetic and copies ran while one was open for 8% of the time, Pallas kernels for 0%

commit v1 on v0

--- a/solution.py
+++ b/solution.py
@@ -109,7 +109,7 @@
     )
     results, grad_in, grad_out = lax.map(run_expert, (arrived, arrived_grads, exp_in, exp_out))
     returned = lax.all_to_all(results, "exp", split_axis=1, concat_axis=0, tiled=True)
-    grad_in, grad_out = lax.psum((grad_in, grad_out), ("lat", "dp"))
+    grad_in, grad_out = lax.psum(lax.psum((grad_in, grad_out), "dp"), "lat")
     expert_out = jnp.dot(
         placer.T, returned.reshape(EXPERTS * CAP, block_width), preferred_element_type=jnp.float32
     ).astype(jnp.bfloat16)

time: 1640 us -> 802 us (0.49)
  waiting for transfers between devices: 1290 us -> 459 us
    psum x1 -> x2, waiting for transfers between devices: 1240 us -> 394 us  [body(): grad_in, grad_out = lax.psum(lax.psum((grad_in, grad_out), 'dp'), 'lat')]
  transfers between devices with their start and end apart: 6 -> 7, of which waited for: 3 -> 4; matrix products, arithmetic and copies ran while one was open for 8% -> 17% of each run, Pallas kernels for 0% -> 0%
where the time goes in v1:
time: 802 us; the launch traced here: 791 us
  waiting for transfers between devices  459 us (57%)
  matrix products  161 us (20%)
  local copies, waits for them, and re-layouts  101 us (13%)
  other arithmetic  35 us (4%)
  starting transfers between devices  21.1 us (3%)
  between operations  14.5 us (2%)
    psum x2, waiting for transfers between devices, body(): grad_in, grad_out = lax.psum(lax.psum((grad_in, grad_out), 'dp'), 'lat')  394 us
    dot_general x8, matrix products, expert_pass(): pre_act = jnp.dot(inputs, w_in, preferred_element_type=jnp.float32)  58.7 us
    dot_general x1, matrix products, dense_block(): reduced = jnp.dot(active, w_reduce, preferred_element_type=jnp.float32)  42.4 us
    all_to_all x1, waiting for transfers between devices, body(): lax.all_to_all(results, 'exp', split_axis=1, concat_axis=0, tiled=True)  37.3 us
    dot_general x8, matrix products, expert_pass(): grad_in = jnp.dot(inputs.T, scaled, preferred_element_type=jnp.float32)  31 us
    all_to_all x1, waiting for transfers between devices, body(): lax.all_to_all(outgoing, 'exp', split_axis=0, concat_axis=1, tiled=True)  27.1 us
    reduce_sum x1, other arithmetic, dense_block(): channel_mean = jnp.mean(smoothed, axis=-1, keepdims=True)  26.9 us
    dynamic_slice x16, local copies, waits for them, and re-layouts, body(): lax.map(run_expert, (arrived, arrived_grads, exp_in, exp_out))  22.6 us
  transfers between devices with their start and end apart: 7, of which 4 were waited for; matrix products, arithmetic and copies ran while one was open for 17% of the time, Pallas kernels for 0%

profile of v1, /device:TPU:7, one launch (start us, length us, event | category | flops | bytes accessed | tf_op | source)
XLA Modules:
  0.0 791.3 jit_solution(1799531077816769084)
XLA Ops:
  10.3 5.5 collective-permute-start.1
  17.0 2.7 copy.24
  19.8 3.2 reshape.261
  23.0 2.2 convolution_convert_fusion.1
  25.1 2.5 reshape.262
  27.6 5.9 all-to-all-start.1
  36.3 2.2 fusion.69
  38.6 26.9 %fusion.104 = (f32[16,256]{1,0:T(8,128)S(1)}, f32[1,16,256,192]{2,3,1,0:T(8,128)S(1)}) fusion(f32[192]{0:T(256)S(1)} %bitcast.171, bf16[1,22,262,192]{2,3,1,0:T(8,128)(2,1)S(1)} %fusion.69, f32[192]{0:T(256)S(1)} %bitcast.172, f32[192]{0:T(256)S(1)} %bitcast.144, f32[192]{0:T(256)S(1)} %bitcast.145, ...), kind=kLoop, calls=%fused_computation.138 | loop fusion | flops 115601408 | bytes 80270080 | tf_op jit(solution)/shard_map/reduce_sum | solution.py:48
  68.6 42.4 %fusion.60 = bf16[4096,192]{0,1:T(8,128)(2,1)} fusion(f32[4096,192]{0,1:T(8,128)S(1)} %bitcast.141, bf16[768,192]{0,1:T(8,128)(2,1)S(1)} %copy-done, bf16[4096,192]{0,1:T(8,128)(2,1)} %bitcast.142, bf16[192,768]{1,0:T(8,128)(2,1)} %param.16), kind=kOutput, calls=%fused_computation.83 | convolution fusion | flops 2621964288 | bytes 6881280 | tf_op jit(solution)/shard_map/dot_general | solution.py:55
  110.9 3.2 copy.22
  114.1 3.2 reshape_reshape.3
  119.5 2.5 reshape.260
  122.0 4.0 all-to-all-start
  126.0 3.6 copy.25
  129.6 3.0 copy.27
  132.6 27.1 %all-to-all-done = bf16[16,3,24576]{2,1,0:T(4,128)(2,1)S(1)} async-done(((bf16[16,3,24576]{2,1,0:T(4,128)(2,1)}), bf16[16,3,24576]{2,1,0:T(4,128)(2,1)S(1)}, u32[]{:S(2)}, u32[]{:S(2)}) %all-to-all-start) | async-done | bytes 2359328 | tf_op jit(solution)/shard_map/all_to_all | solution.py:107
  161.4 3.0 copy.26
  164.4 147.8 %while.14 = (s32[]{:T(128)}, bf16[8,6,24576]{2,1,0:T(8,128)(2,1)}, f32[8,192,768]{2,1,0:T(8,128)}, f32[8,768,192]{1,2,0:T(8,128)}, bf16[8,6,24576]{2,1,0:T(8,128...) while((s32[]{:T(128)}, bf16[8,6,24576]{2,1,0:T(8,128)(2,1)}, ...), condition=%wide.region_5.6_spmd, body=%wide.region_4.5_spmd.sunk | while | flops 1176846336 | bytes 16123001 | solution.py:110
  166.3 7.3 fusion.141
  178.1 3.9 fusion.142
  184.7 7.3 fusion.141
  196.5 3.9 fusion.142
  203.1 7.3 fusion.141
  214.9 3.9 fusion.142
  221.6 7.3 fusion.141
  233.3 3.9 fusion.142
  240.0 7.3 fusion.141
  251.8 3.9 fusion.142
  258.4 7.3 fusion.141
  270.2 3.9 fusion.142
  276.8 7.3 fusion.141
  288.6 3.9 fusion.142
  295.3 7.3 fusion.141
  307.0 3.9 fusion.142
  312.3 211.2 %all-reduce.6.cloned.1.call-done = (f32[8,192,768]{2,1,0:T(8,128)}, f32[8,768,192]{1,2,0:T(8,128)}) async-done(((f32[8,192,768]{2,1,0:T(8,128)}, f32[8,768,192]{1,2,0:T(8,128)}), (f32[8,192,768]{2,1,0:T(8,128)}, f32[8,768,192]{1,2,0:T(8,128)})) %all-reduce.6.cloned.1.call-update) | async-done | bytes 9437200 | tf_op jit(solution)/shard_map/psum | solution.py:112
  525.3 2.7 copy.28
  528.0 4.4 all-to-all-start.2
  532.4 4.2 copy.32
  536.6 37.3 %all-to-all-done.2 = bf16[8,6,24576]{2,0,1:T(8,128)(2,1)S(1)} async-done(((bf16[8,6,24576]{2,0,1:T(8,128)(2,1)}), bf16[8,6,24576]{2,0,1:T(8,128)(2,1)S(1)}, u32[]{:S(2)}, u32[]{:S(2)}) %all-to-all-start.2) | async-done | bytes 2359328 | tf_op jit(solution)/shard_map/all_to_all | solution.py:111
  575.3 3.8 copy.29
  579.1 3.0 reshape.263
  582.1 2.3 fusion.43
  584.3 3.2 reshape.266
  587.6 4.1 add_convert_fusion
  591.7 2.3 copy.31
  593.9 183.1 %all-reduce.8.cloned.1.call-done = (f32[8,192,768]{2,1,0:T(8,128)}, f32[8,768,192]{1,2,0:T(8,128)}) async-done(((f32[8,192,768]{2,1,0:T(8,128)}, f32[8,768,192]{1,2,0:T(8,128)}), (f32[8,192,768]{2,1,0:T(8,128)}, f32[8,768,192]{1,2,0:T(8,128)})) %all-reduce.8.cloned.1.call-update) | async-done | bytes 9437200 | tf_op jit(solution)/shard_map/psum | solution.py:112
  777.1 5.0 copy.62
  782.1 2.2 copy.63
  (117 shorter events, 74.9 us)
Async XLA Ops:
  7.2 60.9 %copy-start = (bf16[768,192]{0,1:T(8,128)(2,1)S(1)}, bf16[768,192]{0,1:T(8,128)(2,1)}, u32[]{:S(2)}) copy-start(bf16[768,192]{0,1:T(8,128)(2,1)} %param.17) | copy-start | bytes 884740
  9.0 24.5 %collective-permute-start = (bf16[1,3,256,192]{2,3,1,0:T(8,128)(2,1)}, bf16[1,3,256,192]{2,3,1,0:T(8,128)(2,1)S(1)}, u32[]{:S(2)}, u32[]{:S(2)}) collective-permute-start(bf16[1,3,256,192]{2,3,1,0:T(8,128)(2,1)} %get-tuple-element.90), channel_id=1, source_target_pairs={{0,128},{1,129},{2,130},{3,131},{4,132},{5,133},{6,134},{7,135},{8... | collective-permute-start | bytes 884744 | tf_op jit(solution)/shard_map/ppermute | solution.py:16
  10.3 26.0 %collective-permute-start.1 = (bf16[1,3,256,192]{2,3,1,0:T(8,128)(2,1)S(1)}, bf16[1,3,256,192]{2,3,1,0:T(8,128)(2,1)S(1)}, u32[]{:S(2)}, u32[]{:S(2)}) collective-permute-start(bf16[1,3,256,192]{2,3,1,0:T(8,128)(2,1)S(1)} %get-tuple-element.91), channel_id=1, source_target_pairs={{128,0},{129,1},{130,2},{131,3},{132,4},{133,5},{134,6},{135,7},{1... | collective-permute-start | bytes 884744 | tf_op jit(solution)/shard_map/ppermute | solution.py:19
  27.6 5.9 copy-start.6
  27.6 6.0 copy-start.2
  27.6 94.4 %all-to-all-start.1 = ((bf16[16,3,24576]{2,1,0:T(4,128)(2,1)}), bf16[16,3,24576]{2,1,0:T(4,128)(2,1)}, u32[]{:S(2)}, u32[]{:S(2)}) async-start(bf16[16,3,24576]{2,1,0:T(4,128)(2,1)} %reshape.262), calls=%async_computation.1 | async-start | bytes 6291456 | tf_op jit(solution)/shard_map/all_to_all | solution.py:108
  65.5 0.7 copy-start.7
  66.2 2.4 copy-start.4
  122.0 37.7 %all-to-all-start = ((bf16[16,3,24576]{2,1,0:T(4,128)(2,1)}), bf16[16,3,24576]{2,1,0:T(4,128)(2,1)S(1)}, u32[]{:S(2)}, u32[]{:S(2)}) async-start(bf16[16,3,24576]{2,1,0:T(4,128)(2,1)} %reshape.260), calls=%async_computation | async-start | bytes 6291456 | tf_op jit(solution)/shard_map/all_to_all | solution.py:107
  126.0 397.5 %all-reduce.6.cloned.1.call-start = ((), (), s32[]{:S(2)}) async-start(), calls=%async_computation.3 | async-start | bytes 18874368 | tf_op jit(solution)/shard_map/psum | solution.py:112
  312.2 464.9 %all-reduce.8.cloned.1.call-start = ((), (), s32[]{:S(2)}) async-start(), calls=%async_computation.4 | async-start | bytes 18874368 | tf_op jit(solution)/shard_map/psum | solution.py:112
  523.4 1.9 copy-start.5
  528.0 45.8 %all-to-all-start.2 = ((bf16[8,6,24576]{2,0,1:T(8,128)(2,1)}), bf16[8,6,24576]{2,0,1:T(8,128)(2,1)S(1)}, u32[]{:S(2)}, u32[]{:S(2)}) async-start(bf16[8,6,24576]{2,0,1:T(8,128)(2,1)} %copy.28), calls=%async_computation.2 | async-start | bytes 4718592 | tf_op jit(solution)/shard_map/all_to_all | solution.py:111
  573.9 1.4 copy-start.3
  777.1 5.0 slice-start
  777.1 5.0 slice-start.1
  777.1 7.2 copy-start.1
Sparse Core Ops, SparseCore 0:
  312.3 211.0 all-reduce.5
  526.5 250.5 all-reduce.7

commit v2 on v1

--- a/solution.py
+++ b/solution.py
@@ -2,6 +2,8 @@
 import jax.numpy as jnp
 from jax import lax
 from jax.sharding import PartitionSpec as P
+from jax.experimental import pallas as pl
+from jax.experimental.pallas import tpu as pltpu
 
 EXPERTS = 16
 BLOCK = 128
@@ -20,6 +22,101 @@
         block = jnp.concatenate([low, block, high], axis=dim)
     return block
 
+
+def reduce_plan(lat_size, dp_size):
+    dp_bits = dp_size.bit_length() - 1
+    rest = list(range(1, dp_bits))
+    other = rest[2:] + rest[:2] if len(rest) > 2 else rest
+    plan = [("dp", 0, 0)] + [("dp", a, b) for a, b in zip(rest, other)]
+    plan += [("lat", 0, 0)] * (lat_size.bit_length() - 1)
+    return plan
+
+
+def allreduce_kernel(plan, rows, in_ref, out_ref, *scratch):
+    stages = len(plan)
+    bufs = scratch[:stages]
+    sums = scratch[stages:2 * stages]
+    rs_send, rs_recv, ag_send, ag_recv = scratch[2 * stages:]
+    lat = lax.axis_index("lat")
+    dp = lax.axis_index("dp")
+    ex = lax.axis_index("exp")
+    core = dp % 2
+
+    bits, partners = [], []
+    for axis, b0, b1 in plan:
+        me = dp if axis == "dp" else lat
+        bit = jnp.where(core == 0, (me // (1 << b0)) % 2, (me // (1 << b1)) % 2)
+        step = jnp.where(core == 0, 1 << b0, 1 << b1)
+        other = me + (1 - 2 * bit) * step
+        bits.append(bit)
+        partners.append((lat, other, ex) if axis == "dp" else (other, dp, ex))
+
+    barrier = pltpu.get_barrier_semaphore()
+    for dev in partners:
+        pl.semaphore_signal(barrier, 1, device_id=dev, device_id_type=pl.DeviceIdType.MESH)
+    pl.semaphore_wait(barrier, stages)
+
+    los = []
+    lo = jnp.int32(0)
+    for k in range(stages):
+        half = rows >> (k + 1)
+        los.append(lo)
+        src = in_ref if k == 0 else sums[k - 1]
+        keep = bits[k] * half
+        give = (1 - bits[k]) * half
+        copy = pltpu.make_async_remote_copy(
+            src_ref=src.at[pl.ds(give, half)],
+            dst_ref=bufs[k],
+            send_sem=rs_send.at[k],
+            recv_sem=rs_recv.at[k],
+            device_id=partners[k],
+            device_id_type=pl.DeviceIdType.MESH,
+        )
+        copy.start()
+        copy.wait()
+        chunk = min(half, 1152)
+
+        def add(i, carry, src=src, keep=keep, chunk=chunk, k=k):
+            at = pl.multiple_of(i * chunk, 8)
+            sums[k][pl.ds(at, chunk)] = src[pl.ds(keep + at, chunk)] + bufs[k][pl.ds(at, chunk)]
+            return carry
+
+        lax.fori_loop(0, half // chunk, add, 0)
+        lo = lo + bits[k] * half
+
+    last = rows >> stages
+    out_ref[pl.ds(lo, last)] = sums[stages - 1][...]
+    for k in reversed(range(stages)):
+        half = rows >> (k + 1)
+        copy = pltpu.make_async_remote_copy(
+            src_ref=out_ref.at[pl.ds(lo, half)],
+            dst_ref=out_ref.at[pl.ds(lo, half)],
+            send_sem=ag_send.at[k],
+            recv_sem=ag_recv.at[k],
+            device_id=partners[k],
+            device_id_type=pl.DeviceIdType.MESH,
+        )
+        copy.start()
+        copy.wait()
+        lo = los[k]
+
+
+def tree_allreduce(flat):
+    rows = flat.shape[0]
+    plan = reduce_plan(lax.axis_size("lat"), lax.axis_size("dp"))
+    stages = len(plan)
+    scratch = [pltpu.VMEM((rows >> (k + 1), 128), jnp.float32) for k in range(stages)] * 2
+    scratch += [pltpu.SemaphoreType.DMA((stages,))] * 4
+    return pl.pallas_call(
+        lambda *refs: allreduce_kernel(plan, rows, *refs),
+        out_shape=jax.ShapeDtypeStruct(flat.shape, flat.dtype),
+        in_specs=[pl.BlockSpec(memory_space=pltpu.VMEM)],
+        out_specs=pl.BlockSpec(memory_space=pltpu.VMEM),
+        scratch_shapes=scratch,
+        compiler_params=pltpu.CompilerParams(
+            collective_id=0, has_side_effects=True, vmem_limit_bytes=62 * 1024 * 1024
+        ),
+    )(flat)
 
 def gelu_slope(values):
     return (
@@ -109,7 +206,11 @@
     )
     results, grad_in, grad_out = lax.map(run_expert, (arrived, arrived_grads, exp_in, exp_out))
     returned = lax.all_to_all(results, "exp", split_axis=1, concat_axis=0, tiled=True)
-    grad_in, grad_out = lax.psum(lax.psum((grad_in, grad_out), "dp"), "lat")
+    flat = jnp.concatenate([grad_in.reshape(-1, 128), grad_out.reshape(-1, 128)])
+    flat = tree_allreduce(flat)
+    half = flat.shape[0] // 2
+    grad_in = flat[:half].reshape(grad_in.shape)
+    grad_out = flat[half:].reshape(grad_out.shape)
     expert_out = jnp.dot(
         placer.T, returned.reshape(EXPERTS * CAP, block_width), preferred_element_type=jnp.float32
     ).astype(jnp.bfloat16)

time: 802 us -> 621 us (0.77)
  waiting for transfers between devices: 459 us -> 23 us
  Pallas kernels: 0 us -> 234 us
  local copies, waits for them, and re-layouts: 101 us -> 136 us
  between operations: 14.5 us -> 1.07 us
  matrix products: 161 us -> 150 us
  other arithmetic: 35 us -> 44.2 us
    psum x2 -> x0, waiting for transfers between devices: 394 us -> none  [body(): grad_in, grad_out = lax.psum(lax.psum((grad_in, grad_out), 'dp'), 'lat')]
    pallas_call x0 -> x1, Pallas kernels: none -> 234 us  [tree_allreduce(): pl.pallas_call(lambda *refs: allreduce_kernel(plan, rows, *refs), out_sha...]
    all_to_all x1, waiting for transfers between devices: 37.3 us -> 0.01 us  [body(): lax.all_to_all(results, 'exp', split_axis=1, concat_axis=0, tiled=True)]
    reshape x0 -> x4, local copies, waits for them, and re-layouts: none -> 26.4 us  [the longest x1 7.79 us: body(): grad_out.reshape(-1, 128)]
    dot_general x1, matrix products: 42.4 us -> 32.2 us  [dense_block(): reduced = jnp.dot(active, w_reduce, preferred_element_type=jnp.float32)]
    concatenate x0 -> x1, other arithmetic: none -> 9.21 us  [body(): jnp.concatenate([grad_in.reshape(-1, 128), grad_out.reshape(-1, 128)])]
    unnamed x28 -> x25, local copies, waits for them, and re-layouts: 20.4 us -> 16.1 us
  transfers between devices with their start and end apart: 7 -> 5, of which waited for: 4 -> 1; matrix products, arithmetic and copies ran while one was open for 17% -> 23% of each run, Pallas kernels for 0% -> 38%
where the time goes in v2:
time: 621 us; the launch traced here: 611 us
  Pallas kernels  234 us (38%)
  matrix products  150 us (24%)
  local copies, waits for them, and re-layouts  136 us (22%)
  other arithmetic  44.2 us (7%)
  waiting for transfers between devices  23 us (4%)
  starting transfers between devices  22.8 us (4%)
    pallas_call x1, Pallas kernels, tree_allreduce(): pl.pallas_call(lambda *refs: allreduce_kernel(plan, rows, *refs), out_sha...  234 us
    dot_general x8, matrix products, expert_pass(): pre_act = jnp.dot(inputs, w_in, preferred_element_type=jnp.float32)  58.2 us
    dot_general x1, matrix products, dense_block(): reduced = jnp.dot(active, w_reduce, preferred_element_type=jnp.float32)  32.2 us
    dot_general x8, matrix products, expert_pass(): grad_in = jnp.dot(inputs.T, scaled, preferred_element_type=jnp.float32)  31 us
    reduce_sum x1, other arithmetic, dense_block(): channel_mean = jnp.mean(smoothed, axis=-1, keepdims=True)  26.9 us
    all_to_all x1, waiting for transfers between devices, body(): lax.all_to_all(outgoing, 'exp', split_axis=0, concat_axis=1, tiled=True)  22.9 us
    dynamic_slice x16, local copies, waits for them, and re-layouts, body(): lax.map(run_expert, (arrived, arrived_grads, exp_in, exp_out))  22.6 us
    unnamed x25, local copies, waits for them, and re-layouts  16.1 us
  transfers between devices with their start and end apart: 5, of which 1 were waited for; matrix products, arithmetic and copies ran while one was open for 23% of the time, Pallas kernels for 38%

profile of v2, /device:TPU:7, one launch (start us, length us, event | category | flops | bytes accessed | tf_op | source)
XLA Modules:
  0.0 611.4 jit_solution(5854460646719884115)
XLA Ops:
  3.8 5.5 collective-permute-start.1
  10.5 2.7 copy.26
  13.2 3.2 reshape.273
  18.6 2.5 reshape.274
  21.1 6.0 all-to-all-start.1
  32.1 26.9 %fusion.104 = (f32[16,256]{1,0:T(8,128)S(1)}, f32[1,16,256,192]{2,3,1,0:T(8,128)S(1)}) fusion(f32[192]{0:T(256)S(1)} %bitcast.168, bf16[1,22,262,192]{2,3,1,0:T(8,128)(2,1)S(1)} %fusion.69, f32[192]{0:T(256)S(1)} %bitcast.169, f32[192]{0:T(256)S(1)} %bitcast.141, f32[192]{0:T(256)S(1)} %bitcast.142, ...), kind=kLoop, calls=%fused_computation.139 | loop fusion | flops 115601408 | bytes 80270080 | tf_op jit(solution)/shard_map/reduce_sum | solution.py:145
  62.1 32.2 %fusion.60 = bf16[4096,192]{0,1:T(8,128)(2,1)} fusion(f32[4096,192]{0,1:T(8,128)S(1)} %bitcast.138, bf16[768,192]{0,1:T(8,128)(2,1)S(1)} %copy-done, bf16[4096,192]{0,1:T(8,128)(2,1)} %bitcast.139, bf16[192,768]{1,0:T(8,128)(2,1)} %param.16), kind=kOutput, calls=%fused_computation.84 | convolution fusion | flops 2621964288 | bytes 6881280 | tf_op jit(solution)/shard_map/dot_general | solution.py:152
  94.3 3.2 copy.24
  97.5 3.2 reshape_reshape.3
  102.8 2.6 reshape.272
  105.4 4.0 all-to-all-start
  109.4 4.1 copy.36
  113.5 3.6 copy.27
  117.1 3.0 copy.29
  120.1 22.9 %all-to-all-done = bf16[16,3,24576]{2,1,0:T(4,128)(2,1)S(1)} async-done(((bf16[16,3,24576]{2,1,0:T(4,128)(2,1)}), bf16[16,3,24576]{2,1,0:T(4,128)(2,1)S(1)}, u32[]{:S(2)}, u32[]{:S(2)}) %all-to-all-start) | async-done | bytes 2359328 | tf_op jit(solution)/shard_map/all_to_all | solution.py:204
  144.8 3.1 copy.28
  147.9 147.0 %while.14 = (s32[]{:T(128)}, bf16[8,6,24576]{2,1,0:T(8,128)(2,1)}, f32[8,192,768]{2,1,0:T(8,128)}, f32[8,768,192]{1,2,0:T(8,128)}, bf16[8,6,24576]{2,1,0:T(8,128...) while((s32[]{:T(128)}, bf16[8,6,24576]{2,1,0:T(8,128)(2,1)}, ...), condition=%wide.region_5.6_spmd, body=%wide.region_4.5_spmd.sunk | while | flops 1176846336 | bytes 16123001 | solution.py:207
  149.4 7.3 %fusion.142 = (bf16[768,768]{1,0:T(8,128)(2,1)S(1)}, f32[768,768]{1,0:T(8,128)}) fusion(bf16[768,192]{1,0:T(8,128)(2,1)S(1)} %reshape.285, bf16[8,192,768]{2,1,0:T(8,128)(2,1)} %get-tuple-element.222, s32[]{:T(128)S(6)} %copy.52), kind=kOutput, calls=%fused_computation.4.clone.1 | convolution fusion | flops 264830976 | bytes 4128772 | tf_op jit(solution)/shard_map/while/body/eval_jaxpr/dot_general | solution.py:158
  161.1 3.9 fusion.143
  167.8 7.3 %fusion.142 = (bf16[768,768]{1,0:T(8,128)(2,1)S(1)}, f32[768,768]{1,0:T(8,128)}) fusion(bf16[768,192]{1,0:T(8,128)(2,1)S(1)} %reshape.285, bf16[8,192,768]{2,1,0:T(8,128)(2,1)} %get-tuple-element.222, s32[]{:T(128)S(6)} %copy.52), kind=kOutput, calls=%fused_computation.4.clone.1 | convolution fusion | flops 264830976 | bytes 4128772 | tf_op jit(solution)/shard_map/while/body/eval_jaxpr/dot_general | solution.py:158
  179.5 3.9 fusion.143
  186.1 7.3 %fusion.142 = (bf16[768,768]{1,0:T(8,128)(2,1)S(1)}, f32[768,768]{1,0:T(8,128)}) fusion(bf16[768,192]{1,0:T(8,128)(2,1)S(1)} %reshape.285, bf16[8,192,768]{2,1,0:T(8,128)(2,1)} %get-tuple-element.222, s32[]{:T(128)S(6)} %copy.52), kind=kOutput, calls=%fused_computation.4.clone.1 | convolution fusion | flops 264830976 | bytes 4128772 | tf_op jit(solution)/shard_map/while/body/eval_jaxpr/dot_general | solution.py:158
  197.9 3.9 fusion.143
  204.5 7.3 %fusion.142 = (bf16[768,768]{1,0:T(8,128)(2,1)S(1)}, f32[768,768]{1,0:T(8,128)}) fusion(bf16[768,192]{1,0:T(8,128)(2,1)S(1)} %reshape.285, bf16[8,192,768]{2,1,0:T(8,128)(2,1)} %get-tuple-element.222, s32[]{:T(128)S(6)} %copy.52), kind=kOutput, calls=%fused_computation.4.clone.1 | convolution fusion | flops 264830976 | bytes 4128772 | tf_op jit(solution)/shard_map/while/body/eval_jaxpr/dot_general | solution.py:158
  216.3 3.9 fusion.143
  222.9 7.3 %fusion.142 = (bf16[768,768]{1,0:T(8,128)(2,1)S(1)}, f32[768,768]{1,0:T(8,128)}) fusion(bf16[768,192]{1,0:T(8,128)(2,1)S(1)} %reshape.285, bf16[8,192,768]{2,1,0:T(8,128)(2,1)} %get-tuple-element.222, s32[]{:T(128)S(6)} %copy.52), kind=kOutput, calls=%fused_computation.4.clone.1 | convolution fusion | flops 264830976 | bytes 4128772 | tf_op jit(solution)/shard_map/while/body/eval_jaxpr/dot_general | solution.py:158
  234.6 3.9 fusion.143
  241.2 7.3 %fusion.142 = (bf16[768,768]{1,0:T(8,128)(2,1)S(1)}, f32[768,768]{1,0:T(8,128)}) fusion(bf16[768,192]{1,0:T(8,128)(2,1)S(1)} %reshape.285, bf16[8,192,768]{2,1,0:T(8,128)(2,1)} %get-tuple-element.222, s32[]{:T(128)S(6)} %copy.52), kind=kOutput, calls=%fused_computation.4.clone.1 | convolution fusion | flops 264830976 | bytes 4128772 | tf_op jit(solution)/shard_map/while/body/eval_jaxpr/dot_general | solution.py:158
  253.0 3.9 fusion.143
  259.6 7.3 %fusion.142 = (bf16[768,768]{1,0:T(8,128)(2,1)S(1)}, f32[768,768]{1,0:T(8,128)}) fusion(bf16[768,192]{1,0:T(8,128)(2,1)S(1)} %reshape.285, bf16[8,192,768]{2,1,0:T(8,128)(2,1)} %get-tuple-element.222, s32[]{:T(128)S(6)} %copy.52), kind=kOutput, calls=%fused_computation.4.clone.1 | convolution fusion | flops 264830976 | bytes 4128772 | tf_op jit(solution)/shard_map/while/body/eval_jaxpr/dot_general | solution.py:158
  271.3 3.9 fusion.143
  278.0 7.3 %fusion.142 = (bf16[768,768]{1,0:T(8,128)(2,1)S(1)}, f32[768,768]{1,0:T(8,128)}) fusion(bf16[768,192]{1,0:T(8,128)(2,1)S(1)} %reshape.285, bf16[8,192,768]{2,1,0:T(8,128)(2,1)} %get-tuple-element.222, s32[]{:T(128)S(6)} %copy.52), kind=kOutput, calls=%fused_computation.4.clone.1 | convolution fusion | flops 264830976 | bytes 4128772 | tf_op jit(solution)/shard_map/while/body/eval_jaxpr/dot_general | solution.py:158
  289.7 3.9 fusion.143
  294.8 6.3 %copy.33 = f32[8,768,192]{2,1,0:T(8,128)} copy(f32[8,768,192]{1,2,0:T(8,128)} %get-tuple-element.49) | data formatting | bytes 9437184 | tf_op jit(solution)/shard_map/while | solution.py:207
  301.1 7.8 %reshape.277 = f32[9216,128]{1,0:T(8,128)} reshape(f32[8,768,192]{2,1,0:T(8,128)} %copy.33) | data formatting | bytes 9437184 | tf_op jit(solution)/shard_map/reshape | solution.py:209
  308.9 2.8 copy.30
  311.7 6.1 all-to-all-start.2
  317.8 5.7 reshape.276
  323.5 9.2 %pad_maximum_fusion.refs_0_ = f32[18432,128]{1,0:T(8,128)} fusion(f32[9216,128]{1,0:T(8,128)} %reshape.277, f32[9216,128]{1,0:T(8,128)} %reshape.276), kind=kLoop, calls=%fused_computation.80 | loop fusion | flops 2359296 | bytes 18874368 | tf_op jit(solution)/shard_map/concatenate | solution.py:209
  332.7 234.4 %shard_map.112 = f32[18432,128]{1,0:T(8,128)} custom-call(f32[18432,128]{1,0:T(8,128)} %pad_maximum_fusion.refs_0_), custom_call_target="tpu_custom_call" | custom-call | tf_op jit(solution)/shard_map/pallas_call | solution.py:110
  567.1 6.5 %fusion.105 = (f32[9216,128]{1,0:T(8,128)}, f32[9216,128]{1,0:T(8,128)}) fusion(f32[18432,128]{1,0:T(8,128)} %shard_map.112), kind=kLoop, calls=%fused_computation.140 | loop fusion | bytes 18874368 | tf_op jit(solution)/shard_map/slice | solution.py:213
  573.6 6.9 %reshape.279 = f32[8,768,192]{2,1,0:T(8,128)} reshape(f32[9216,128]{1,0:T(8,128)} %get-tuple-element.86) | data formatting | bytes 9437184 | tf_op jit(solution)/shard_map/reshape | solution.py:213
  580.5 6.1 copy.35
  586.6 6.0 reshape.278
  592.6 3.7 copy.31
  596.3 3.0 reshape.275
  601.6 3.3 reshape.282
  604.9 4.1 add_convert_fusion
  (115 shorter events, 80.5 us)
Async XLA Ops:
  0.6 61.0 %copy-start = (bf16[768,192]{0,1:T(8,128)(2,1)S(1)}, bf16[768,192]{0,1:T(8,128)(2,1)}, u32[]{:S(2)}) copy-start(bf16[768,192]{0,1:T(8,128)(2,1)} %param.17) | copy-start | bytes 884740
  2.5 24.6 %collective-permute-start = (bf16[1,3,256,192]{2,3,1,0:T(8,128)(2,1)}, bf16[1,3,256,192]{2,3,1,0:T(8,128)(2,1)S(1)}, u32[]{:S(2)}, u32[]{:S(2)}) collective-permute-start(bf16[1,3,256,192]{2,3,1,0:T(8,128)(2,1)} %get-tuple-element.91), channel_id=1, source_target_pairs={{0,128},{1,129},{2,130},{3,131},{4,132},{5,133},{6,134},{7,135},{8... | collective-permute-start | bytes 884744 | tf_op jit(solution)/shard_map/ppermute | solution.py:18
  3.8 26.1 %collective-permute-start.1 = (bf16[1,3,256,192]{2,3,1,0:T(8,128)(2,1)S(1)}, bf16[1,3,256,192]{2,3,1,0:T(8,128)(2,1)S(1)}, u32[]{:S(2)}, u32[]{:S(2)}) collective-permute-start(bf16[1,3,256,192]{2,3,1,0:T(8,128)(2,1)S(1)} %get-tuple-element.92), channel_id=1, source_target_pairs={{128,0},{129,1},{130,2},{131,3},{132,4},{133,5},{134,6},{135,7},{1... | collective-permute-start | bytes 884744 | tf_op jit(solution)/shard_map/ppermute | solution.py:21
  10.5 90.2 %copy-start.6 = (s32[32]{0:T(128)}, s32[32]{0:T(128)S(1)}, u32[]{:S(2)}) copy-start(s32[32]{0:T(128)S(1)} %add_add_fusion) | copy-start | bytes 388
  21.1 6.0 copy-start.5
  21.1 6.1 copy-start.2
  21.1 84.3 %all-to-all-start.1 = ((bf16[16,3,24576]{2,1,0:T(4,128)(2,1)}), bf16[16,3,24576]{2,1,0:T(4,128)(2,1)}, u32[]{:S(2)}, u32[]{:S(2)}) async-start(bf16[16,3,24576]{2,1,0:T(4,128)(2,1)} %reshape.274), calls=%async_computation.1 | async-start | bytes 6291456 | tf_op jit(solution)/shard_map/all_to_all | solution.py:205
  59.0 0.7 copy-start.8
  59.7 2.4 copy-start.3
  105.4 37.7 %all-to-all-start = ((bf16[16,3,24576]{2,1,0:T(4,128)(2,1)}), bf16[16,3,24576]{2,1,0:T(4,128)(2,1)S(1)}, u32[]{:S(2)}, u32[]{:S(2)}) async-start(bf16[16,3,24576]{2,1,0:T(4,128)(2,1)} %reshape.272), calls=%async_computation | async-start | bytes 6291456 | tf_op jit(solution)/shard_map/all_to_all | solution.py:204
  301.1 7.8 %copy-start.4 = (bf16[8,6,24576]{2,1,0:T(8,128)(2,1)S(1)}, bf16[8,6,24576]{2,1,0:T(8,128)(2,1)}, u32[]{:S(2)}) copy-start(bf16[8,6,24576]{2,1,0:T(8,128)(2,1)} %get-tuple-element.47) | copy-start | bytes 7077892
  311.7 280.9 %all-to-all-start.2 = ((bf16[8,6,24576]{2,0,1:T(8,128)(2,1)}), bf16[8,6,24576]{2,0,1:T(8,128)(2,1)}, u32[]{:S(2)}, u32[]{:S(2)}) async-start(bf16[8,6,24576]{2,0,1:T(8,128)(2,1)} %copy.30), calls=%async_computation.2 | async-start | bytes 4718592 | tf_op jit(solution)/shard_map/all_to_all | solution.py:208
  596.3 3.1 copy-start.7
  604.9 6.3 %copy-start.1 = (bf16[768,192]{0,1:T(8,128)(2,1)S(1)}, bf16[768,192]{0,1:T(8,128)(2,1)}, u32[]{:S(2)}) copy-start(bf16[768,192]{0,1:T(8,128)(2,1)} %param.17) | copy-start | bytes 884740

commit v3 on v2

--- a/solution.py
+++ b/solution.py
@@ -36,7 +36,9 @@
     stages = len(plan)
     bufs = scratch[:stages]
     sums = scratch[stages:2 * stages]
-    rs_send, rs_recv, ag_send, ag_recv = scratch[2 * stages:]
+    staged = scratch[2 * stages:3 * stages]
+    gathered = scratch[3 * stages]
+    rs_send, rs_recv, ag_send, ag_recv = scratch[3 * stages + 1:]
     lat = lax.axis_index("lat")
     dp = lax.axis_index("dp")
     ex = lax.axis_index("exp")
@@ -56,6 +58,10 @@
         pl.semaphore_signal(barrier, 1, device_id=dev, device_id_type=pl.DeviceIdType.MESH)
     pl.semaphore_wait(barrier, stages)
 
+    def chunked(count, body):
+        chunk = min(count, 1152)
+        lax.fori_loop(0, count // chunk, lambda i, c: (body(pl.multiple_of(i * chunk, 16), chunk), c)[1], 0)
+
     los = []
     lo = jnp.int32(0)
     for k in range(stages):
@@ -64,8 +70,13 @@
         src = in_ref if k == 0 else sums[k - 1]
         keep = bits[k] * half
         give = (1 - bits[k]) * half
+
+        def narrow(at, chunk, src=src, give=give, k=k):
+            staged[k][pl.ds(at, chunk)] = src[pl.ds(pl.multiple_of(give + at, 16), chunk)].astype(jnp.bfloat16)
+
+        chunked(half, narrow)
         copy = pltpu.make_async_remote_copy(
-            src_ref=src.at[pl.ds(give, half)],
+            src_ref=staged[k],
             dst_ref=bufs[k],
             send_sem=rs_send.at[k],
             recv_sem=rs_recv.at[k],
@@ -74,23 +85,23 @@
         )
         copy.start()
         copy.wait()
-        chunk = min(half, 1152)
-
-        def add(i, carry, src=src, keep=keep, chunk=chunk, k=k):
-            at = pl.multiple_of(i * chunk, 8)
-            sums[k][pl.ds(at, chunk)] = src[pl.ds(keep + at, chunk)] + bufs[k][pl.ds(at, chunk)]
-            return carry
-
-        lax.fori_loop(0, half // chunk, add, 0)
+
+        def add(at, chunk, src=src, keep=keep, k=k):
+            sums[k][pl.ds(at, chunk)] = src[pl.ds(pl.multiple_of(keep + at, 16), chunk)] + bufs[k][
+                pl.ds(at, chunk)
+            ].astype(jnp.float32)
+
+        chunked(half, add)
         lo = lo + bits[k] * half
 
     last = rows >> stages
-    out_ref[pl.ds(lo, last)] = sums[stages - 1][...]
+    lo = pl.multiple_of(lo, 16)
+    gathered[pl.ds(lo, last)] = sums[stages - 1][...].astype(jnp.bfloat16)
     for k in reversed(range(stages)):
         half = rows >> (k + 1)
         copy = pltpu.make_async_remote_copy(
-            src_ref=out_ref.at[pl.ds(lo, half)],
-            dst_ref=out_ref.at[pl.ds(lo, half)],
+            src_ref=gathered.at[pl.ds(pl.multiple_of(lo, 16), half)],
+            dst_ref=gathered.at[pl.ds(pl.multiple_of(lo, 16), half)],
             send_sem=ag_send.at[k],
             recv_sem=ag_recv.at[k],
             device_id=partners[k],
@@ -100,12 +111,20 @@
         copy.wait()
         lo = los[k]
 
+    def widen_out(at, chunk):
+        out_ref[pl.ds(at, chunk)] = gathered[pl.ds(at, chunk)].astype(jnp.float32)
+
+    chunked(rows, widen_out)
+
 
 def tree_allreduce(flat):
     rows = flat.shape[0]
     plan = reduce_plan(lax.axis_size("lat"), lax.axis_size("dp"))
     stages = len(plan)
-    scratch = [pltpu.VMEM((rows >> (k + 1), 128), jnp.float32) for k in range(stages)] * 2
+    scratch = [pltpu.VMEM((rows >> (k + 1), 128), jnp.bfloat16) for k in range(stages)]
+    scratch += [pltpu.VMEM((rows >> (k + 1), 128), jnp.float32) for k in range(stages)]
+    scratch += [pltpu.VMEM((rows >> (k + 1), 128), jnp.bfloat16) for k in range(stages)]
+    scratch += [pltpu.VMEM((rows, 128), jnp.bfloat16)]
     scratch += [pltpu.SemaphoreType.DMA((stages,))] * 4
     return pl.pallas_call(
         lambda *refs: allreduce_kernel(plan, rows, *refs),

time: 621 us -> 529 us (0.85)
  Pallas kernels: 234 us -> 143 us
    pallas_call x1, Pallas kernels: 234 us -> 143 us  [tree_allreduce(): pl.pallas_call(lambda *refs: allreduce_kernel(plan, rows, *refs), out_sha...]
  transfers between devices with their start and end apart: 5 -> 5, of which waited for: 1 -> 1; matrix products, arithmetic and copies ran while one was open for 23% -> 27% of each run, Pallas kernels for 38% -> 27%
where the time goes in v3:
time: 529 us; the launch traced here: 520 us
  matrix products  150 us (28%)
  Pallas kernels  143 us (27%)
  local copies, waits for them, and re-layouts  136 us (26%)
  other arithmetic  44.2 us (8%)
  waiting for transfers between devices  23 us (4%)
  starting transfers between devices  22.8 us (4%)
    pallas_call x1, Pallas kernels, tree_allreduce(): pl.pallas_call(lambda *refs: allreduce_kernel(plan, rows, *refs), out_sha...  143 us
    dot_general x8, matrix products, expert_pass(): pre_act = jnp.dot(inputs, w_in, preferred_element_type=jnp.float32)  58.2 us
    dot_general x1, matrix products, dense_block(): reduced = jnp.dot(active, w_reduce, preferred_element_type=jnp.float32)  32.2 us
    dot_general x8, matrix products, expert_pass(): grad_in = jnp.dot(inputs.T, scaled, preferred_element_type=jnp.float32)  31 us
    reduce_sum x1, other arithmetic, dense_block(): channel_mean = jnp.mean(smoothed, axis=-1, keepdims=True)  26.9 us
    all_to_all x1, waiting for transfers between devices, body(): lax.all_to_all(outgoing, 'exp', split_axis=0, concat_axis=1, tiled=True)  22.9 us
    dynamic_slice x16, local copies, waits for them, and re-layouts, body(): lax.map(run_expert, (arrived, arrived_grads, exp_in, exp_out))  22.6 us
    unnamed x25, local copies, waits for them, and re-layouts  16.1 us
  transfers between devices with their start and end apart: 5, of which 1 were waited for; matrix products, arithmetic and copies ran while one was open for 27% of the time, Pallas kernels for 27%

profile of v3, /device:TPU:7, one launch (start us, length us, event | category | flops | bytes accessed | tf_op | source)
XLA Modules:
  0.0 519.9 jit_solution(3313984082308383634)
XLA Ops:
  3.8 5.5 %collective-permute-start.1 = (bf16[1,3,256,192]{2,3,1,0:T(8,128)(2,1)S(1)}, bf16[1,3,256,192]{2,3,1,0:T(8,128)(2,1)S(1)}, u32[]{:S(2)}, u32[]{:S(2)}) collective-permute-start(bf16[1,3,256,192]{2,3,1,0:T(8,128)(2,1)S(1)} %get-tuple-element.92), channel_id=1, source_target_pairs={{128,0},{129,1},{130,2},{131,3},{132,4},{133,5},{134,6},{135,7},{1... | collective-permute-start | bytes 884744 | tf_op jit(solution)/shard_map/ppermute | solution.py:21
  10.5 2.7 copy.26
  13.2 3.2 reshape.273
  18.6 2.5 reshape.274
  21.1 6.0 %all-to-all-start.1 = ((bf16[16,3,24576]{2,1,0:T(4,128)(2,1)}), bf16[16,3,24576]{2,1,0:T(4,128)(2,1)}, u32[]{:S(2)}, u32[]{:S(2)}) async-start(bf16[16,3,24576]{2,1,0:T(4,128)(2,1)} %reshape.274), calls=%async_computation.1 | async-start | bytes 6291456 | tf_op jit(solution)/shard_map/all_to_all | solution.py:224
  32.1 26.9 %fusion.104 = (f32[16,256]{1,0:T(8,128)S(1)}, f32[1,16,256,192]{2,3,1,0:T(8,128)S(1)}) fusion(f32[192]{0:T(256)S(1)} %bitcast.168, bf16[1,22,262,192]{2,3,1,0:T(8,128)(2,1)S(1)} %fusion.69, f32[192]{0:T(256)S(1)} %bitcast.169, f32[192]{0:T(256)S(1)} %bitcast.141, f32[192]{0:T(256)S(1)} %bitcast.142, ...), kind=kLoop, calls=%fused_computation.139 | loop fusion | flops 115601408 | bytes 80270080 | tf_op jit(solution)/shard_map/reduce_sum | solution.py:164
  62.1 32.2 %fusion.60 = bf16[4096,192]{0,1:T(8,128)(2,1)} fusion(f32[4096,192]{0,1:T(8,128)S(1)} %bitcast.138, bf16[768,192]{0,1:T(8,128)(2,1)S(1)} %copy-done, bf16[4096,192]{0,1:T(8,128)(2,1)} %bitcast.139, bf16[192,768]{1,0:T(8,128)(2,1)} %param.16), kind=kOutput, calls=%fused_computation.84 | convolution fusion | flops 2621964288 | bytes 6881280 | tf_op jit(solution)/shard_map/dot_general | solution.py:171
  94.3 3.2 copy.24
  97.5 3.2 reshape_reshape.3
  102.8 2.6 reshape.272
  105.4 4.0 all-to-all-start
  109.4 4.1 copy.36
  113.5 3.6 copy.27
  117.1 3.0 copy.29
  120.1 22.9 %all-to-all-done = bf16[16,3,24576]{2,1,0:T(4,128)(2,1)S(1)} async-done(((bf16[16,3,24576]{2,1,0:T(4,128)(2,1)}), bf16[16,3,24576]{2,1,0:T(4,128)(2,1)S(1)}, u32[]{:S(2)}, u32[]{:S(2)}) %all-to-all-start) | async-done | bytes 2359328 | tf_op jit(solution)/shard_map/all_to_all | solution.py:223
  144.8 3.1 copy.28
  147.9 147.0 %while.14 = (s32[]{:T(128)}, bf16[8,6,24576]{2,1,0:T(8,128)(2,1)}, f32[8,192,768]{2,1,0:T(8,128)}, f32[8,768,192]{1,2,0:T(8,128)}, bf16[8,6,24576]{2,1,0:T(8,128...) while((s32[]{:T(128)}, bf16[8,6,24576]{2,1,0:T(8,128)(2,1)}, ...), condition=%wide.region_5.6_spmd, body=%wide.region_4.5_spmd.sunk | while | flops 1176846336 | bytes 16123001 | solution.py:226
  149.4 7.3 %fusion.142 = (bf16[768,768]{1,0:T(8,128)(2,1)S(1)}, f32[768,768]{1,0:T(8,128)}) fusion(bf16[768,192]{1,0:T(8,128)(2,1)S(1)} %reshape.285, bf16[8,192,768]{2,1,0:T(8,128)(2,1)} %get-tuple-element.222, s32[]{:T(128)S(6)} %copy.52), kind=kOutput, calls=%fused_computation.4.clone.1 | convolution fusion | flops 264830976 | bytes 4128772 | tf_op jit(solution)/shard_map/while/body/eval_jaxpr/dot_general | solution.py:177
  161.1 3.9 fusion.143
  167.8 7.3 %fusion.142 = (bf16[768,768]{1,0:T(8,128)(2,1)S(1)}, f32[768,768]{1,0:T(8,128)}) fusion(bf16[768,192]{1,0:T(8,128)(2,1)S(1)} %reshape.285, bf16[8,192,768]{2,1,0:T(8,128)(2,1)} %get-tuple-element.222, s32[]{:T(128)S(6)} %copy.52), kind=kOutput, calls=%fused_computation.4.clone.1 | convolution fusion | flops 264830976 | bytes 4128772 | tf_op jit(solution)/shard_map/while/body/eval_jaxpr/dot_general | solution.py:177
  179.5 3.9 fusion.143
  186.1 7.3 %fusion.142 = (bf16[768,768]{1,0:T(8,128)(2,1)S(1)}, f32[768,768]{1,0:T(8,128)}) fusion(bf16[768,192]{1,0:T(8,128)(2,1)S(1)} %reshape.285, bf16[8,192,768]{2,1,0:T(8,128)(2,1)} %get-tuple-element.222, s32[]{:T(128)S(6)} %copy.52), kind=kOutput, calls=%fused_computation.4.clone.1 | convolution fusion | flops 264830976 | bytes 4128772 | tf_op jit(solution)/shard_map/while/body/eval_jaxpr/dot_general | solution.py:177
  197.9 3.9 fusion.143
  204.5 7.3 %fusion.142 = (bf16[768,768]{1,0:T(8,128)(2,1)S(1)}, f32[768,768]{1,0:T(8,128)}) fusion(bf16[768,192]{1,0:T(8,128)(2,1)S(1)} %reshape.285, bf16[8,192,768]{2,1,0:T(8,128)(2,1)} %get-tuple-element.222, s32[]{:T(128)S(6)} %copy.52), kind=kOutput, calls=%fused_computation.4.clone.1 | convolution fusion | flops 264830976 | bytes 4128772 | tf_op jit(solution)/shard_map/while/body/eval_jaxpr/dot_general | solution.py:177
  216.3 3.9 fusion.143
  222.9 7.3 %fusion.142 = (bf16[768,768]{1,0:T(8,128)(2,1)S(1)}, f32[768,768]{1,0:T(8,128)}) fusion(bf16[768,192]{1,0:T(8,128)(2,1)S(1)} %reshape.285, bf16[8,192,768]{2,1,0:T(8,128)(2,1)} %get-tuple-element.222, s32[]{:T(128)S(6)} %copy.52), kind=kOutput, calls=%fused_computation.4.clone.1 | convolution fusion | flops 264830976 | bytes 4128772 | tf_op jit(solution)/shard_map/while/body/eval_jaxpr/dot_general | solution.py:177
  234.6 3.9 fusion.143
  241.2 7.3 %fusion.142 = (bf16[768,768]{1,0:T(8,128)(2,1)S(1)}, f32[768,768]{1,0:T(8,128)}) fusion(bf16[768,192]{1,0:T(8,128)(2,1)S(1)} %reshape.285, bf16[8,192,768]{2,1,0:T(8,128)(2,1)} %get-tuple-element.222, s32[]{:T(128)S(6)} %copy.52), kind=kOutput, calls=%fused_computation.4.clone.1 | convolution fusion | flops 264830976 | bytes 4128772 | tf_op jit(solution)/shard_map/while/body/eval_jaxpr/dot_general | solution.py:177
  253.0 3.9 fusion.143
  259.6 7.3 %fusion.142 = (bf16[768,768]{1,0:T(8,128)(2,1)S(1)}, f32[768,768]{1,0:T(8,128)}) fusion(bf16[768,192]{1,0:T(8,128)(2,1)S(1)} %reshape.285, bf16[8,192,768]{2,1,0:T(8,128)(2,1)} %get-tuple-element.222, s32[]{:T(128)S(6)} %copy.52), kind=kOutput, calls=%fused_computation.4.clone.1 | convolution fusion | flops 264830976 | bytes 4128772 | tf_op jit(solution)/shard_map/while/body/eval_jaxpr/dot_general | solution.py:177
  271.3 3.9 fusion.143
  278.0 7.3 %fusion.142 = (bf16[768,768]{1,0:T(8,128)(2,1)S(1)}, f32[768,768]{1,0:T(8,128)}) fusion(bf16[768,192]{1,0:T(8,128)(2,1)S(1)} %reshape.285, bf16[8,192,768]{2,1,0:T(8,128)(2,1)} %get-tuple-element.222, s32[]{:T(128)S(6)} %copy.52), kind=kOutput, calls=%fused_computation.4.clone.1 | convolution fusion | flops 264830976 | bytes 4128772 | tf_op jit(solution)/shard_map/while/body/eval_jaxpr/dot_general | solution.py:177
  289.7 3.9 fusion.143
  294.8 6.3 %copy.33 = f32[8,768,192]{2,1,0:T(8,128)} copy(f32[8,768,192]{1,2,0:T(8,128)} %get-tuple-element.49) | data formatting | bytes 9437184 | tf_op jit(solution)/shard_map/while | solution.py:226
  301.1 7.8 %reshape.277 = f32[9216,128]{1,0:T(8,128)} reshape(f32[8,768,192]{2,1,0:T(8,128)} %copy.33) | data formatting | bytes 9437184 | tf_op jit(solution)/shard_map/reshape | solution.py:228
  308.9 2.8 copy.30
  311.7 6.1 %all-to-all-start.2 = ((bf16[8,6,24576]{2,0,1:T(8,128)(2,1)}), bf16[8,6,24576]{2,0,1:T(8,128)(2,1)}, u32[]{:S(2)}, u32[]{:S(2)}) async-start(bf16[8,6,24576]{2,0,1:T(8,128)(2,1)} %copy.30), calls=%async_computation.2 | async-start | bytes 4718592 | tf_op jit(solution)/shard_map/all_to_all | solution.py:227
  317.8 5.7 %reshape.276 = f32[9216,128]{1,0:T(8,128)} reshape(f32[8,192,768]{2,1,0:T(8,128)} %get-tuple-element.48) | data formatting | bytes 9437184 | tf_op jit(solution)/shard_map/reshape | solution.py:228
  323.5 9.2 %pad_maximum_fusion.refs_0_ = f32[18432,128]{1,0:T(8,128)} fusion(f32[9216,128]{1,0:T(8,128)} %reshape.277, f32[9216,128]{1,0:T(8,128)} %reshape.276), kind=kLoop, calls=%fused_computation.80 | loop fusion | flops 2359296 | bytes 18874368 | tf_op jit(solution)/shard_map/concatenate | solution.py:228
  332.7 142.9 %shard_map.112 = f32[18432,128]{1,0:T(8,128)} custom-call(f32[18432,128]{1,0:T(8,128)} %pad_maximum_fusion.refs_0_), custom_call_target="tpu_custom_call" | custom-call | tf_op jit(solution)/shard_map/pallas_call | solution.py:129
  475.6 6.5 %fusion.105 = (f32[9216,128]{1,0:T(8,128)}, f32[9216,128]{1,0:T(8,128)}) fusion(f32[18432,128]{1,0:T(8,128)} %shard_map.112), kind=kLoop, calls=%fused_computation.140 | loop fusion | bytes 18874368 | tf_op jit(solution)/shard_map/slice | solution.py:232
  482.1 6.9 %reshape.279 = f32[8,768,192]{2,1,0:T(8,128)} reshape(f32[9216,128]{1,0:T(8,128)} %get-tuple-element.86) | data formatting | bytes 9437184 | tf_op jit(solution)/shard_map/reshape | solution.py:232
  489.0 6.1 %copy.35 = f32[8,768,192]{1,2,0:T(8,128)} copy(f32[8,768,192]{2,1,0:T(8,128)} %reshape.279) | data formatting | bytes 9437184
  495.1 6.0 %reshape.278 = f32[8,192,768]{2,1,0:T(8,128)} reshape(f32[9216,128]{1,0:T(8,128)} %get-tuple-element.87) | data formatting | bytes 9437184 | tf_op jit(solution)/shard_map/reshape | solution.py:231
  501.1 3.7 copy.31
  504.8 3.0 reshape.275
  510.1 3.3 reshape.282
  513.4 4.1 add_convert_fusion
  (115 shorter events, 80.5 us)
Async XLA Ops:
  0.6 61.0 %copy-start = (bf16[768,192]{0,1:T(8,128)(2,1)S(1)}, bf16[768,192]{0,1:T(8,128)(2,1)}, u32[]{:S(2)}) copy-start(bf16[768,192]{0,1:T(8,128)(2,1)} %param.17) | copy-start | bytes 884740
  2.5 24.6 %collective-permute-start = (bf16[1,3,256,192]{2,3,1,0:T(8,128)(2,1)}, bf16[1,3,256,192]{2,3,1,0:T(8,128)(2,1)S(1)}, u32[]{:S(2)}, u32[]{:S(2)}) collective-permute-start(bf16[1,3,256,192]{2,3,1,0:T(8,128)(2,1)} %get-tuple-element.91), channel_id=1, source_target_pairs={{0,128},{1,129},{2,130},{3,131},{4,132},{5,133},{6,134},{7,135},{8... | collective-permute-start | bytes 884744 | tf_op jit(solution)/shard_map/ppermute | solution.py:18
  3.8 26.1 %collective-permute-start.1 = (bf16[1,3,256,192]{2,3,1,0:T(8,128)(2,1)S(1)}, bf16[1,3,256,192]{2,3,1,0:T(8,128)(2,1)S(1)}, u32[]{:S(2)}, u32[]{:S(2)}) collective-permute-start(bf16[1,3,256,192]{2,3,1,0:T(8,128)(2,1)S(1)} %get-tuple-element.92), channel_id=1, source_target_pairs={{128,0},{129,1},{130,2},{131,3},{132,4},{133,5},{134,6},{135,7},{1... | collective-permute-start | bytes 884744 | tf_op jit(solution)/shard_map/ppermute | solution.py:21
  10.5 90.2 %copy-start.6 = (s32[32]{0:T(128)}, s32[32]{0:T(128)S(1)}, u32[]{:S(2)}) copy-start(s32[32]{0:T(128)S(1)} %add_add_fusion) | copy-start | bytes 388
  21.1 6.0 %copy-start.5 = (f32[7,7,192]{2,1,0:T(8,128)S(1)}, f32[7,7,192]{2,1,0:T(8,128)}, u32[]{:S(2)}) copy-start(f32[7,7,192]{2,1,0:T(8,128)} %param.14) | copy-start | bytes 112900
  21.1 6.1 %copy-start.2 = (bf16[1,16,256,192]{2,3,1,0:T(8,128)(2,1)S(1)}, bf16[1,16,256,192]{2,3,1,0:T(8,128)(2,1)}, u32[]{:S(2)}) copy-start(bf16[1,16,256,192]{2,3,1,0:T(8,128)(2,1)} %param.11) | copy-start | bytes 4718596
  21.1 84.3 %all-to-all-start.1 = ((bf16[16,3,24576]{2,1,0:T(4,128)(2,1)}), bf16[16,3,24576]{2,1,0:T(4,128)(2,1)}, u32[]{:S(2)}, u32[]{:S(2)}) async-start(bf16[16,3,24576]{2,1,0:T(4,128)(2,1)} %reshape.274), calls=%async_computation.1 | async-start | bytes 6291456 | tf_op jit(solution)/shard_map/all_to_all | solution.py:224
  59.0 0.7 copy-start.8
  59.7 2.4 copy-start.3
  105.4 37.7 %all-to-all-start = ((bf16[16,3,24576]{2,1,0:T(4,128)(2,1)}), bf16[16,3,24576]{2,1,0:T(4,128)(2,1)S(1)}, u32[]{:S(2)}, u32[]{:S(2)}) async-start(bf16[16,3,24576]{2,1,0:T(4,128)(2,1)} %reshape.272), calls=%async_computation | async-start | bytes 6291456 | tf_op jit(solution)/shard_map/all_to_all | solution.py:223
  301.1 7.8 %copy-start.4 = (bf16[8,6,24576]{2,1,0:T(8,128)(2,1)S(1)}, bf16[8,6,24576]{2,1,0:T(8,128)(2,1)}, u32[]{:S(2)}) copy-start(bf16[8,6,24576]{2,1,0:T(8,128)(2,1)} %get-tuple-element.47) | copy-start | bytes 7077892
  311.7 189.4 %all-to-all-start.2 = ((bf16[8,6,24576]{2,0,1:T(8,128)(2,1)}), bf16[8,6,24576]{2,0,1:T(8,128)(2,1)}, u32[]{:S(2)}, u32[]{:S(2)}) async-start(bf16[8,6,24576]{2,0,1:T(8,128)(2,1)} %copy.30), calls=%async_computation.2 | async-start | bytes 4718592 | tf_op jit(solution)/shard_map/all_to_all | solution.py:227
  504.8 3.1 copy-start.7
  513.4 6.3 %copy-start.1 = (bf16[768,192]{0,1:T(8,128)(2,1)S(1)}, bf16[768,192]{0,1:T(8,128)(2,1)}, u32[]{:S(2)}) copy-start(bf16[768,192]{0,1:T(8,128)(2,1)} %param.17) | copy-start | bytes 884740
